TPU v7x, 128 devices: a whole 4x4x4 slice. The times are simulated.
128 devices in a mesh: tm: 8 (over y_lo, x), space: 16 (over y_hi, z, core).
Axes of the slice: x: 4, y: 4 (y_hi: 2, y_lo: 2; y = y_hi * 2 + y_lo), z: 4, core: 2. Of those that a mesh axis runs over, the one named last changes fastest.
Arguments:
- frames_in: bfloat16 [32, 64, 64, 512], P('tm', 'space'), may hold values from -6 to 6
- spatial_kernel: bfloat16 [3, 3, 512, 512], replicated, may hold values from -0.09375 to 0.09375
- temporal_kernel: bfloat16 [3, 512, 512], replicated, may hold values from -0.15625 to 0.15625
- norm_gain: float32 [512], replicated, may hold values from 0.1 to 1.9
- query_weight: bfloat16 [512, 512], replicated, may hold values from -2 to 2
- key_weight: bfloat16 [512, 512], replicated, may hold values from -2 to 2
- value_weight: bfloat16 [512, 512], replicated, may hold values from -0.25 to 0.25
- out_weight: bfloat16 [512, 512], replicated, may hold values from -0.25 to 0.25
- cotangent: bfloat16 [32, 64, 64, 512], P('tm', 'space'), may hold values from -6 to 6
Outputs:
- encoded: bfloat16 [32, 64, 64, 512], P('tm', 'space')
- kernel_grad: float32 [3, 512, 512], P(None, 'tm', 'space')
All inputs are finite; a program needn't handle non-finite values.
Results may differ from a plain program's by a relative error of at most 0.007.
Values may be sent and summed in bfloat16 or wider, within the bound.
A program may use at most 128 MiB of HBM per device.

v0:
```python
import jax
import jax.numpy as jnp
from jax import lax
from jax.sharding import PartitionSpec as P


def extended_2(cells, sides, width):
    for axis, dim in sides:
        count = lax.axis_size(axis)
        ends = count - 1
        head = lax.slice_in_dim(cells, 0, width, axis=dim)
        tail = lax.slice_in_dim(cells, cells.shape[dim] - width, cells.shape[dim], axis=dim)
        cells = jnp.concatenate(
            [
                lax.ppermute(tail, axis, [(i, (i + 1) % count) for i in range(ends)]),
                cells,
                lax.ppermute(head, axis, [((i + 1) % count, i) for i in range(ends)]),
            ],
            axis=dim,
        )
    return cells


def from_behind(value, axis, steps):
    count = lax.axis_size(axis)
    first, last = (max(0, -steps), min(count, count - steps))
    return lax.ppermute(value, axis, [(source, source + steps) for source in range(first, last)])


def project_all(normed, query_weight, key_weight, value_weight, lead, positions, chans):
    query = (
        jnp.dot(normed, query_weight, preferred_element_type=jnp.float32)
        .astype(jnp.bfloat16)
        .reshape(lead, positions, chans)
    )
    key = (
        jnp.dot(normed, key_weight, preferred_element_type=jnp.float32)
        .astype(jnp.bfloat16)
        .reshape(lead, positions, chans)
    )
    value = (
        jnp.dot(normed, value_weight, preferred_element_type=jnp.float32)
        .astype(jnp.bfloat16)
        .reshape(lead, positions, chans)
    )
    return (query, key, value)


def on_device(
    frames_in,
    spatial_kernel,
    temporal_kernel,
    norm_gain,
    query_weight,
    key_weight,
    value_weight,
    out_weight,
    cotangent,
):
    frames, rows, cols, chans = frames_in.shape
    padded = extended_2(frames_in, (("space", 1),), 1)
    padded = jnp.pad(padded, ((0, 0), (0, 0), (1, 1), (0, 0)))
    spatial = jnp.zeros((frames * rows * cols, chans), jnp.float32)
    for di in range(3):
        for dj in range(3):
            piece = padded[:, di : di + rows, dj : dj + cols, :].reshape(-1, chans)
            spatial = spatial + jnp.dot(
                piece, spatial_kernel[di, dj], preferred_element_type=jnp.float32
            )
    act = jax.nn.silu(spatial).astype(jnp.bfloat16).reshape(frames, rows, cols, chans)
    earlier = from_behind(act[frames - 2 :], "tm", 1)
    extended = jnp.concatenate([earlier, act], axis=0)
    temporal = jnp.zeros((frames * rows * cols, chans), jnp.float32)
    flat_grad = cotangent.reshape(-1, chans)
    grads = []
    for tap in range(3):
        shifted = extended[2 - tap : 2 - tap + frames].reshape(-1, chans)
        temporal = temporal + jnp.dot(
            shifted, temporal_kernel[tap], preferred_element_type=jnp.float32
        )
        grads.append(
            jnp.einsum("nc,nd->cd", shifted, flat_grad, preferred_element_type=jnp.float32)
        )
    partial_grad = jnp.stack(grads, axis=0)
    hidden = (frames_in.reshape(-1, chans).astype(jnp.float32) + temporal).astype(jnp.bfloat16)
    wide = hidden.astype(jnp.float32)
    normed = (
        wide / jnp.sqrt(jnp.mean(wide * wide, axis=1, keepdims=True) + 1e-06) * norm_gain
    ).astype(jnp.bfloat16)
    positions = rows * cols
    query, key, value = project_all(
        normed, query_weight, key_weight, value_weight, frames, positions, chans
    )
    first_frame = lax.axis_index("tm") * frames
    query_frames = first_frame + jnp.arange(frames)
    scale = 1.0 / jnp.sqrt(jnp.float32(chans))
    running_max = jnp.full((frames, positions), -1e30, jnp.float32)
    key_piece = lax.all_gather(key, "tm", axis=0, tiled=True)
    value_piece = lax.all_gather(value, "tm", axis=0, tiled=True)
    scores = (
        jnp.einsum("anc,bnc->abn", query, key_piece, preferred_element_type=jnp.float32) * scale
    )
    key_frames = jnp.arange(key_piece.shape[0])
    allowed = (key_frames[None, :] <= query_frames[:, None])[:, :, None]
    masked = jnp.where(allowed, scores, jnp.float32(-1e30))
    new_max = jnp.maximum(running_max, jnp.max(masked, axis=1))
    expon = jnp.where(allowed, jnp.exp(scores - new_max[:, None, :]), jnp.float32(0.0))
    new_sum = jnp.sum(expon, axis=1)
    new_acc = jnp.einsum("abn,bnc->anc", expon, value_piece.astype(jnp.float32))
    attended = (new_acc / new_sum[:, :, None]).astype(jnp.bfloat16)
    encoded = (
        wide + jnp.dot(attended.reshape(-1, chans), out_weight, preferred_element_type=jnp.float32)
    ).astype(jnp.bfloat16)
    section = lax.psum_scatter(partial_grad, "space", scatter_dimension=2, tiled=True)
    kernel_grad = lax.psum_scatter(section, "tm", scatter_dimension=1, tiled=True)
    return (encoded.reshape(frames, rows, cols, chans), kernel_grad)


def solution(mesh):
    in_specs = (
        P("tm", "space", None, None),
        P(),
        P(),
        P(),
        P(),
        P(),
        P(),
        P(),
        P("tm", "space", None, None),
    )
    out_specs = (P("tm", "space", None, None), P(None, "tm", "space"))
    return jax.shard_map(
        on_device, mesh=mesh, in_specs=in_specs, out_specs=out_specs, check_vma=False
    )
```

profile of v0, /device:TPU:0, one launch (start us, length us, event | category | flops | bytes accessed | tf_op | source)
XLA Modules:
  0.0 464.2 jit_solution(18101736379835137255)
XLA Ops:
  7.2 0.0 copy-start
  7.2 0.0 all-reduce.4.cloned.1.call-start
  7.2 1.1 fusion.74
  8.4 0.0 copy-start.2
  8.4 1.4 collective-permute-start
  9.8 1.3 collective-permute-start.1
  11.1 2.1 fusion.41
  13.2 2.3 collective-permute-done.1
  15.5 0.9 fusion.14
  16.4 0.0 slice-start.1
  16.4 1.3 fusion.73
  17.8 0.2 slice-done.1
  18.0 0.7 fusion.37
  18.7 0.7 fusion.39
  19.4 0.7 fusion.43
  20.1 0.7 fusion.45
  20.8 0.7 fusion.49
  21.5 0.2 pad_maximum_fusion.3
  21.7 0.7 fusion.35
  22.4 0.7 fusion.47
  23.1 1.6 multiply_convert_fusion
  24.8 3.4 collective-permute-start.2
  28.2 0.7 convolution_bitcast_fusion
  29.0 7.7 %collective-permute-done.2 = bf16[2,4,64,512]{3,2,1,0:T(8,128)(2,1)S(1)} collective-permute-done((bf16[2,4,64,512]{3,2,1,0:T(8,128)(2,1)S(1)}, bf16[2,4,64,512]{3,2,1,0:T(8,128)(2,1)S(1)}, u32[]{:S(2)}, u32[]{:S(2)}) %collective-permute-start.2) | collective-permute-done | bytes 524320 | tf_op jit(solution)/shard_map/ppermute | solution.py:27
  36.6 0.7 convolution_bitcast_fusion.2
  37.3 0.1 copy-done.4
  37.4 0.7 convolution_bitcast_fusion.1
  38.1 2.0 pad_maximum_fusion
  40.1 5.1 %copy.30 = f32[3,512,512]{1,0,2:T(4,128)} copy(f32[3,512,512]{2,1,0:T(8,128)} %pad_maximum_fusion) | data formatting | bytes 6291456 | tf_op jit(solution)/shard_map/stack | solution.py:84
  45.2 0.0 all-reduce.4.cloned.1.call-update
  45.3 0.2 reduce-scatter.4.cloned.1.call-start
  45.5 0.4 copy-done.10
  45.9 0.6 dynamic-slice
  47.1 1.7 fusion.29
  48.9 1.4 fusion.24
  50.3 0.2 copy-done.3
  50.5 0.7 fusion.27
  51.2 1.0 fusion.5
  52.2 153.0 %all-reduce.4.cloned.1.call-done = f32[3,512,512]{1,0,2:T(4,128)} async-done(((f32[3,512,512]{1,0,2:T(4,128)}), f32[3,512,512]{1,0,2:T(4,128)}) %all-reduce.4.cloned.1.call-update) | async-done | bytes 3145744
  205.2 1.0 constant_dynamic-slice_fusion
  206.2 7.6 %copy.34 = f32[3,512,32]{0,2,1:T(8,128)} copy(f32[3,512,32]{1,0,2:T(4,128)S(1)} %constant_dynamic-slice_fusion) | data formatting | bytes 393216
  213.8 8.8 %reshape.117 = f32[512,96]{1,0:T(8,128)} reshape(f32[512,32,3]{2,1,0:T(8,128)} %bitcast.105) | data formatting | bytes 393216
  222.6 0.0 reduce-scatter.4.cloned.1.call-update
  222.7 0.0 all-gather.5.cloned.1.call-start
  222.7 0.0 copy-start.6
  222.8 1.8 convolution_convert_fusion.1
  224.5 0.0 all-gather.5.cloned.1.call-update
  224.5 0.0 copy-start.7
  224.6 0.3 all-gather.3.cloned.1.call-start
  224.8 1.8 convolution_convert_fusion.2
  226.6 0.0 all-gather.3.cloned.1.call-update
  226.6 0.1 iota_compare_fusion.2
  226.7 1.7 convolution_convert_fusion
  228.4 32.2 %reduce-scatter.4.cloned.1.call-done = f32[64,96]{1,0:T(8,128)} async-done(((f32[512,96]{1,0:T(8,128)}), f32[64,96]{1,0:T(8,128)}) %reduce-scatter.4.cloned.1.call-update) | async-done | bytes 24592
  260.6 1.8 reshape.118
  262.4 1.2 copy.31
  263.7 89.4 %all-gather.5.cloned.1.call-done = bf16[32,256,512]{2,1,0:T(8,128)(2,1)} async-done(((bf16[4,256,512]{2,1,0:T(8,128)(2,1)}), bf16[32,256,512]{2,1,0:T(8,128)(2,1)}) %all-gather.5.cloned.1.call-update) | async-done | bytes 8388624 | tf_op jit(solution)/shard_map/all_gather | solution.py:98
  353.1 9.0 %select_reduce_fusion = (f32[4,256]{0,1:T(8,128)S(1)}, f32[4,32,256]{1,0,2:T(4,128)S(1)}) fusion(pred[4,32]{1,0:T(4,128)(4,1)S(1)} %iota_compare_fusion.2, bf16[4,256,512]{2,1,0:T(8,128)(2,1)} %bitcast.128, bf16[32,256,512]{2,1,0:T(8,128)(2,1)} %all-gather.5.cloned.1.call-done), kind=kOutput, calls=%fused_computation.66 | convolution fusion | flops 33651712 | bytes 9572480 | tf_op jit(solution)/shard_map/anc,bnc->abn/dot_general | solution.py:101
  362.1 0.7 fusion.63
  362.7 83.2 %all-gather.3.cloned.1.call-done = bf16[32,256,512]{2,1,0:T(8,128)(2,1)} async-done(((bf16[4,256,512]{2,1,0:T(8,128)(2,1)}), bf16[32,256,512]{2,1,0:T(8,128)(2,1)}) %all-gather.3.cloned.1.call-update) | async-done | bytes 8388624 | tf_op jit(solution)/shard_map/all_gather | solution.py:99
  445.9 9.0 %fusion.9 = bf16[4,256,512]{2,0,1:T(4,128)(2,1)S(1)} fusion(bf16[32,256,512]{2,1,0:T(8,128)(2,1)} %all-gather.3.cloned.1.call-done, f32[4,256]{0,1:T(8,128)S(1)} %fusion.63, f32[4,32,256]{1,0,2:T(4,128)S(1)} %get-tuple-element.25, f32[4,256]{0,1:T(8,128)S(1)} %broadcast_maximum_fusion, pred[4,32]{1,0:T(4,128)(4,1)S(1)} %iota_compare_fusion.2), kind=kOutput, calls=%fused_computation.21 | convolution fusion | flops 34668544 | bytes 9576576 | tf_op jit(solution)/shard_map/abn,bnc->anc/dot_general | solution.py:109
  455.0 0.2 copy.29
  455.2 0.8 copy-done.8
  456.0 1.7 fusion.8
  (22 shorter events, 0.1 us)
Async XLA Ops:
  7.2 21.0 %copy-start = (bf16[4,4,64,512]{3,2,1,0:T(8,128)(2,1)S(1)}, bf16[4,4,64,512]{3,2,1,0:T(8,128)(2,1)}, u32[]{:S(2)}) copy-start(bf16[4,4,64,512]{3,2,1,0:T(8,128)(2,1)} %param.17) | copy-start | bytes 3145732
  7.2 198.1 %all-reduce.4.cloned.1.call-start = ((), (), s32[]{:S(2)}) async-start(), calls=%async_computation.4 | async-start | bytes 8388608
  8.4 7.1 %copy-start.2 = (bf16[4,4,64,512]{3,2,1,0:T(8,128)(2,1)S(1)}, bf16[4,4,64,512]{3,2,1,0:T(8,128)(2,1)}, u32[]{:S(2)}) copy-start(bf16[4,4,64,512]{3,2,1,0:T(8,128)(2,1)} %param.9) | copy-start | bytes 3145732
  8.4 4.8 %collective-permute-start = (bf16[4,1,64,512]{3,2,1,0:T(8,128)(2,1)S(1)}, bf16[4,1,64,512]{3,2,1,0:T(8,128)(2,1)S(1)}, u32[]{:S(2)}, u32[]{:S(2)}) collective-permute-start(bf16[4,1,64,512]{3,2,1,0:T(8,128)(2,1)S(1)} %get-tuple-element.20), channel_id=1, source_target_pairs={{0,1},{1,2},{2,3},{3,4},{4,5},{5,6},{6,7},{7,8},{8,9},{9,10},{10,1... | collective-permute-start | bytes 786440 | tf_op jit(solution)/shard_map/ppermute | solution.py:15
  9.8 5.7 %collective-permute-start.1 = (bf16[4,1,64,512]{3,2,1,0:T(8,128)(2,1)S(1)}, bf16[4,1,64,512]{3,2,1,0:T(8,128)(2,1)S(1)}, u32[]{:S(2)}, u32[]{:S(2)}) collective-permute-start(bf16[4,1,64,512]{3,2,1,0:T(8,128)(2,1)S(1)} %get-tuple-element.21), channel_id=1, source_target_pairs={{1,0},{2,1},{3,2},{4,3},{5,4},{6,5},{7,6},{8,7},{9,8},{10,9},{11,1... | collective-permute-start | bytes 786440 | tf_op jit(solution)/shard_map/ppermute | solution.py:17
  15.5 2.3 slice-start
  16.4 1.6 slice-start.1
  24.8 11.8 %collective-permute-start.2 = (bf16[2,4,64,512]{3,2,1,0:T(8,128)(2,1)S(1)}, bf16[2,4,64,512]{3,2,1,0:T(8,128)(2,1)S(1)}, u32[]{:S(2)}, u32[]{:S(2)}) collective-permute-start(bf16[2,4,64,512]{3,2,1,0:T(8,128)(2,1)S(1)} %bitcast.127), channel_id=1, source_target_pairs={{0,16},{16,32},{32,48},{48,64},{64,80},{80,96},{96,112},{1,17},{17... | collective-permute-start | bytes 1572872 | tf_op jit(solution)/shard_map/ppermute | solution.py:27
  36.6 0.8 copy-start.4
  45.2 0.7 copy-start.10
  45.3 215.3 %reduce-scatter.4.cloned.1.call-start = ((), (), s32[]{:S(2)}) async-start(), calls=%async_computation.3 | async-start | bytes 294912
  48.9 1.6 copy-start.3
  213.8 8.9 %copy-start.5 = (bf16[512,512]{1,0:T(8,128)(2,1)S(1)}, bf16[512,512]{1,0:T(8,128)(2,1)}, u32[]{:S(2)}) copy-start(bf16[512,512]{1,0:T(8,128)(2,1)} %param.14) | copy-start | bytes 1572868
  213.8 8.9 %copy-start.9 = (f32[512]{0:T(512)S(1)}, f32[512]{0:T(512)}, u32[]{:S(2)}) copy-start(f32[512]{0:T(512)} %param.12) | copy-start | bytes 6148
  222.7 130.4 %all-gather.5.cloned.1.call-start = ((), (), s32[]{:S(2)}) async-start(), calls=%async_computation.2 | async-start | bytes 9437184 | tf_op jit(solution)/shard_map/all_gather | solution.py:98
  222.7 2.1 copy-start.6
  224.5 2.2 copy-start.7
  224.6 221.4 %all-gather.3.cloned.1.call-start = ((), (), s32[]{:S(2)}) async-start(), calls=%async_computation.1 | async-start | bytes 9437184 | tf_op jit(solution)/shard_map/all_gather | solution.py:99
  454.9 1.0 copy-start.8
  455.0 2.7 copy-start.1
Sparse Core Ops, SparseCore 0:
  45.4 159.8 all-reduce.3
  222.8 37.7 reduce-scatter.3
  262.3 90.6 all-gather.4
  355.2 90.6 all-gather.2
where the time goes:
time: 466 us; the launch traced here: 464 us
  waiting for transfers between devices  368 us (79%)
  matrix products  39.1 us (8%)
  local copies, waits for them, and re-layouts  30.6 us (7%)
  between operations  14.7 us (3%)
  starting transfers between devices  6.72 us (1%)
  other arithmetic  5.3 us (1%)
    unnamed x6, waiting for transfers between devices  185 us
    all_gather x1, waiting for transfers between devices, on_device(): key_piece = lax.all_gather(key, 'tm', axis=0, tiled=True)  89.4 us
    all_gather x1, waiting for transfers between devices, on_device(): value_piece = lax.all_gather(value, 'tm', axis=0, tiled=True)  83.2 us
    unnamed x32, local copies, waits for them, and re-layouts  22.8 us
  transfers between devices with their start and end apart: 7, of which 6 were waited for; matrix products, arithmetic and copies ran while one was open for 6% of the time, Pallas kernels for 0%

commit v1 on v0

--- a/solution.py
+++ b/solution.py
@@ -83,36 +83,43 @@
         )
     partial_grad = jnp.stack(grads, axis=0)
     hidden = (frames_in.reshape(-1, chans).astype(jnp.float32) + temporal).astype(jnp.bfloat16)
-    wide = hidden.astype(jnp.float32)
+    parts = lax.axis_size("tm")
+    all_frames = frames * parts
+    positions = rows * cols // parts
+    moved = lax.all_to_all(
+        hidden.reshape(frames, parts * positions, chans), "tm", 1, 0, tiled=True
+    ).reshape(all_frames * positions, chans)
+    wide = moved.astype(jnp.float32)
     normed = (
         wide / jnp.sqrt(jnp.mean(wide * wide, axis=1, keepdims=True) + 1e-06) * norm_gain
     ).astype(jnp.bfloat16)
-    positions = rows * cols
     query, key, value = project_all(
-        normed, query_weight, key_weight, value_weight, frames, positions, chans
+        normed, query_weight, key_weight, value_weight, all_frames, positions, chans
     )
-    first_frame = lax.axis_index("tm") * frames
-    query_frames = first_frame + jnp.arange(frames)
     scale = 1.0 / jnp.sqrt(jnp.float32(chans))
-    running_max = jnp.full((frames, positions), -1e30, jnp.float32)
-    key_piece = lax.all_gather(key, "tm", axis=0, tiled=True)
-    value_piece = lax.all_gather(value, "tm", axis=0, tiled=True)
-    scores = (
-        jnp.einsum("anc,bnc->abn", query, key_piece, preferred_element_type=jnp.float32) * scale
+    scores = jnp.einsum("anc,bnc->nab", query, key, preferred_element_type=jnp.float32) * scale
+    order = jnp.arange(all_frames)
+    allowed = (order[None, :] <= order[:, None])[None, :, :]
+    masked = jnp.where(allowed, scores, jnp.float32(-1e30))
+    expon = jnp.where(
+        allowed, jnp.exp(scores - jnp.max(masked, axis=2, keepdims=True)), jnp.float32(0.0)
     )
-    key_frames = jnp.arange(key_piece.shape[0])
-    allowed = (key_frames[None, :] <= query_frames[:, None])[:, :, None]
-    masked = jnp.where(allowed, scores, jnp.float32(-1e30))
-    new_max = jnp.maximum(running_max, jnp.max(masked, axis=1))
-    expon = jnp.where(allowed, jnp.exp(scores - new_max[:, None, :]), jnp.float32(0.0))
-    new_sum = jnp.sum(expon, axis=1)
-    new_acc = jnp.einsum("abn,bnc->anc", expon, value_piece.astype(jnp.float32))
-    attended = (new_acc / new_sum[:, :, None]).astype(jnp.bfloat16)
+    share = (expon / jnp.sum(expon, axis=2, keepdims=True)).astype(jnp.bfloat16)
+    attended = jnp.einsum("nab,bnc->anc", share, value, preferred_element_type=jnp.float32).astype(
+        jnp.bfloat16
+    )
     encoded = (
         wide + jnp.dot(attended.reshape(-1, chans), out_weight, preferred_element_type=jnp.float32)
     ).astype(jnp.bfloat16)
-    section = lax.psum_scatter(partial_grad, "space", scatter_dimension=2, tiled=True)
-    kernel_grad = lax.psum_scatter(section, "tm", scatter_dimension=1, tiled=True)
+    encoded = lax.all_to_all(
+        encoded.reshape(all_frames, positions, chans), "tm", 0, 1, tiled=True
+    )
+    over = lax.axis_size("space")
+    blocks = partial_grad.reshape(3, parts, chans // parts, over, chans // over)
+    blocks = blocks.transpose(3, 1, 0, 2, 4).reshape(-1, chans)
+    section = lax.psum_scatter(blocks, "space", scatter_dimension=0, tiled=True)
+    kernel_grad = lax.psum_scatter(section, "tm", scatter_dimension=0, tiled=True)
+    kernel_grad = kernel_grad.reshape(3, chans // parts, chans // over)
     return (encoded.reshape(frames, rows, cols, chans), kernel_grad)
 
 

time: 466 us -> 215 us (0.46)
  waiting for transfers between devices: 368 us -> 63.3 us
  blocking collectives: 0 us -> 22.2 us
  local copies, waits for them, and re-layouts: 30.6 us -> 49 us
  starting transfers between devices: 6.72 us -> 23.4 us
  matrix products: 39.1 us -> 30.1 us
    unnamed x6 -> x3, waiting for transfers between devices: 185 us -> 0.02 us
    all_gather x2 -> x0, waiting for transfers between devices: 173 us -> none  [the longest x1 89.4 us: on_device(): key_piece = lax.all_gather(key, 'tm', axis=0, tiled=True)]
    reduce_scatter x0 -> x1, waiting for transfers between devices: none -> 44.8 us  [on_device(): section = lax.psum_scatter(blocks, 'space', scatter_dimension=0, tiled=True)]
    unnamed x0 -> x1, blocking collectives: none -> 22.2 us
    unnamed x32 -> x39, local copies, waits for them, and re-layouts: 22.8 us -> 3.95 us
    all_to_all x0 -> x2, waiting for transfers between devices: none -> 16.3 us  [the longest x1 16.3 us: on_device(): lax.all_to_all(hidden.reshape(frames, parts * positions, chans), 'tm', 1,...]
    dot_general x2, matrix products: 18 us -> 4.45 us  [the longest x1 3.22 us: on_device(): jnp.einsum('nab,bnc->anc', share, value, preferred_element_type=jnp.float32)]
    reshape x0 -> x3, local copies, waits for them, and re-layouts: none -> 11.8 us  [the longest x1 9.94 us: on_device(): blocks = blocks.transpose(3, 1, 0, 2, 4).reshape(-1, chans)]
  transfers between devices with their start and end apart: 7 -> 8, of which waited for: 6 -> 3; matrix products, arithmetic and copies ran while one was open for 6% -> 27% of each run, Pallas kernels for 0% -> 0%
where the time goes in v1:
time: 215 us; the launch traced here: 212 us
  waiting for transfers between devices  63.3 us (29%)
  local copies, waits for them, and re-layouts  49 us (23%)
  matrix products  30.1 us (14%)
  starting transfers between devices  23.4 us (11%)
  blocking collectives  22.2 us (10%)
  between operations  15 us (7%)
  other arithmetic  8.55 us (4%)
    reduce_scatter x1, waiting for transfers between devices, on_device(): section = lax.psum_scatter(blocks, 'space', scatter_dimension=0, tiled=True)  44.8 us
    unnamed x1, blocking collectives  22.2 us
    all_to_all x1, waiting for transfers between devices, on_device(): lax.all_to_all(hidden.reshape(frames, parts * positions, chans), 'tm', 1,...  16.3 us
    another operation x4, local copies, waits for them, and re-layouts, on_device(): partial_grad = jnp.stack(grads, axis=0)  11.1 us
    dot_general x9, matrix products, on_device(): jnp.dot(piece, spatial_kernel[di, dj], preferred_element_type=jnp.float32)  9.96 us
    reshape x1, local copies, waits for them, and re-layouts, on_device(): blocks = blocks.transpose(3, 1, 0, 2, 4).reshape(-1, chans)  9.94 us
    transpose x1, local copies, waits for them, and re-layouts, on_device(): blocks = blocks.transpose(3, 1, 0, 2, 4).reshape(-1, chans)  9.61 us
    all_to_all x1, starting transfers between devices, on_device(): lax.all_to_all(hidden.reshape(frames, parts * positions, chans), 'tm', 1,...  6.21 us
  transfers between devices with their start and end apart: 8, of which 3 were waited for; matrix products, arithmetic and copies ran while one was open for 27% of the time, Pallas kernels for 0%

profile of v1, /device:TPU:0, one launch (start us, length us, event | category | flops | bytes accessed | tf_op | source)
XLA Modules:
  0.0 211.6 jit_solution(1021419693180330083)
XLA Ops:
  7.2 1.2 fusion.77
  8.4 1.3 collective-permute-start.1
  9.7 3.0 %collective-permute-start = (bf16[4,1,64,512]{3,2,1,0:T(8,128)(2,1)S(1)}, bf16[4,1,64,512]{3,2,1,0:T(8,128)(2,1)S(1)}, u32[]{:S(2)}, u32[]{:S(2)}) collective-permute-start(bf16[4,1,64,512]{3,2,1,0:T(8,128)(2,1)S(1)} %get-tuple-element.22), channel_id=1, source_target_pairs={{0,1},{1,2},{2,3},{3,4},{4,5},{5,6},{6,7},{7,8},{8,9},{9,10},{10,1... | collective-permute-start | bytes 786440 | tf_op jit(solution)/shard_map/ppermute | solution.py:15
  12.8 2.3 %copy.96 = bf16[512,1024]{1,0:T(8,128)(2,1)} copy(bf16[512,1024]{0,1:T(8,128)(2,1)} %bitcast.168) | data formatting | bytes 2097152 | tf_op jit(solution)/shard_map/nc,nd->cd/dot_general | solution.py:82
  15.1 1.7 fusion.40
  16.8 0.9 fusion.14
  17.8 1.3 fusion.76
  19.1 0.2 pad_maximum_fusion.2
  19.4 0.7 fusion.34
  20.1 0.7 fusion.36
  20.8 0.7 fusion.38
  21.5 0.7 fusion.42
  22.2 0.7 fusion.44
  22.9 0.7 fusion.48
  23.6 0.7 fusion.46
  24.3 3.3 %multiply_convert_fusion = (bf16[1024,512]{1,0:T(8,128)(2,1)S(1)}, f32[1024,512]{1,0:T(8,128)S(1)}) fusion(bf16[1024,512]{1,0:T(8,128)(2,1)S(1)} %bitcast.167, bf16[3,3,512,512]{3,2,1,0:T(8,128)(2,1)S(1)} %bitcast.153, f32[1024,512]{1,0:T(8,128)S(1)} %fusion.34, f32[1024,512]{1,0:T(8,128)S(1)} %fusion.36, f32[1024,512]{1,0:T(8,128)S(1)} %fusion.38, ...), kind=kOutput, calls=%fused_computation.20 | convolution fusion | flops 543686656 | bytes 21495808 | tf_op jit(solution)/shard_map/dot_general | solution.py:67
  27.6 0.8 slice.116
  28.4 3.7 %collective-permute-start.2 = (bf16[2,4,64,512]{3,2,1,0:T(8,128)(2,1)}, bf16[2,4,64,512]{3,2,1,0:T(8,128)(2,1)S(1)}, u32[]{:S(2)}, u32[]{:S(2)}) collective-permute-start(bf16[2,4,64,512]{3,2,1,0:T(8,128)(2,1)} %bitcast.19), channel_id=1, source_target_pairs={{0,16},{16,32},{32,48},{48,64},{64,80},{80,96},{96,112},{1,17},{17... | collective-permute-start | bytes 1572872 | tf_op jit(solution)/shard_map/ppermute | solution.py:27
  32.1 1.5 fusion.9
  33.7 2.3 %copy.95 = bf16[512,1024]{1,0:T(8,128)(2,1)} copy(bf16[512,1024]{0,1:T(8,128)(2,1)} %fusion.9) | data formatting | bytes 2097152 | tf_op jit(solution)/shard_map/convert_element_type | solution.py:70
  36.0 3.2 %fusion.28 = f32[1024,512]{1,0:T(8,128)} fusion(bf16[1024,512]{1,0:T(8,128)(2,1)S(1)} %get-tuple-element.24, bf16[3,512,512]{2,1,0:T(8,128)(2,1)} %param.11), kind=kOutput, calls=%fused_computation.54 | convolution fusion | flops 536870912 | bytes 3670016 | tf_op jit(solution)/shard_map/dot_general | solution.py:78
  39.2 2.6 %convolution_bitcast_fusion = f32[1,8,64,16,32]{2,4,3,1,0:T(8,128)} fusion(bf16[8,64,1024,1]{2,1,3,0:T(8,128)(2,1)S(1)} %bitcast.171, bf16[16,32,1024,1]{2,1,0,3:T(8,128)(2,1)S(1)} %bitcast.169), kind=kOutput, calls=%fused_computation.30 | convolution fusion | flops 536870912 | bytes 3145728 | tf_op jit(solution)/shard_map/nc,nd->cd/dot_general | solution.py:82
  41.8 2.2 %collective-permute-done.2 = bf16[2,4,64,512]{3,2,1,0:T(8,128)(2,1)S(1)} collective-permute-done((bf16[2,4,64,512]{3,2,1,0:T(8,128)(2,1)}, bf16[2,4,64,512]{3,2,1,0:T(8,128)(2,1)S(1)}, u32[]{:S(2)}, u32[]{:S(2)}) %collective-permute-start.2) | collective-permute-done | bytes 524320 | tf_op jit(solution)/shard_map/ppermute | solution.py:27
  44.0 1.7 convolution_bitcast_fusion.1
  45.8 2.8 %stack.11 = f32[1,8,64,16,32]{2,1,4,3,0:T(8,128)} reshape(f32[512,512]{0,1:T(8,128)} %convolution_bitcast_fusion.1) | data formatting | bytes 2097152 | tf_op jit(solution)/shard_map/stack | solution.py:84
  48.5 3.4 %copy.100 = f32[1,8,64,16,32]{2,4,3,1,0:T(8,128)} copy(f32[1,8,64,16,32]{2,1,4,3,0:T(8,128)} %stack.11) | data formatting | bytes 2097152 | tf_op jit(solution)/shard_map/stack | solution.py:84
  51.9 1.7 convolution_bitcast_fusion.2
  53.7 2.8 %stack.10 = f32[1,8,64,16,32]{2,1,4,3,0:T(8,128)} reshape(f32[512,512]{0,1:T(8,128)} %convolution_bitcast_fusion.2) | data formatting | bytes 2097152 | tf_op jit(solution)/shard_map/stack | solution.py:84
  56.4 2.1 %copy.99 = f32[1,8,64,16,32]{2,4,3,1,0:T(8,128)S(1)} copy(f32[1,8,64,16,32]{2,1,4,3,0:T(8,128)} %stack.10) | data formatting | bytes 2097152 | tf_op jit(solution)/shard_map/stack | solution.py:84
  58.7 0.6 copy-done.4
  59.3 3.4 %maximum_bitcast_fusion = f32[16,8,3,64,32]{3,4,0,1,2:T(8,128)} fusion(f32[1,8,64,16,32]{2,4,3,1,0:T(8,128)S(1)} %copy-done.3, f32[1,8,64,16,32]{2,4,3,1,0:T(8,128)S(1)} %copy.99, f32[1,8,64,16,32]{2,4,3,1,0:T(8,128)S(1)} %copy-done.4), kind=kLoop, calls=%fused_computation.1 | loop fusion | flops 1572864 | bytes 6291456 | tf_op jit(solution)/shard_map/transpose | solution.py:119
  62.6 9.6 %copy.101 = f32[16,8,3,64,32]{4,3,2,1,0:T(8,128)} copy(f32[16,8,3,64,32]{3,4,0,1,2:T(8,128)} %maximum_bitcast_fusion) | data formatting | bytes 6291456 | tf_op jit(solution)/shard_map/transpose | solution.py:119
  72.3 9.9 %reshape.149 = f32[1536,512]{1,0:T(8,128)} reshape(f32[16,8,3,64,32]{4,3,2,1,0:T(8,128)} %copy.101) | data formatting | bytes 6291456 | tf_op jit(solution)/shard_map/reshape | solution.py:119
  82.2 0.2 fusion.20
  82.4 1.2 copy-done.5
  83.6 0.7 fusion.26
  84.4 0.9 add_convert_fusion
  85.3 1.8 copy.85
  87.1 6.2 %all-to-all-start = ((bf16[4,256,512]{2,0,1:T(4,128)(2,1)}), bf16[4,256,512]{2,0,1:T(4,128)(2,1)}, u32[]{:S(2)}, u32[]{:S(2)}) async-start(bf16[4,256,512]{2,0,1:T(4,128)(2,1)} %copy.85), calls=%async_computation | async-start | bytes 2097152 | tf_op jit(solution)/shard_map/all_to_all | solution.py:89
  93.3 16.3 %all-to-all-done = bf16[4,256,512]{2,0,1:T(4,128)(2,1)} async-done(((bf16[4,256,512]{2,0,1:T(4,128)(2,1)}), bf16[4,256,512]{2,0,1:T(4,128)(2,1)}, u32[]{:S(2)}, u32[]{:S(2)}) %all-to-all-start) | async-done | bytes 1048608 | tf_op jit(solution)/shard_map/all_to_all | solution.py:89
  109.6 1.6 copy.86
  111.1 1.8 multiply_reduce_fusion
  113.0 0.1 copy.88
  113.1 0.1 sqrt.12
  113.2 0.3 fusion.7
  113.5 0.7 convolution_convert_fusion.1
  114.3 0.3 copy-done.13
  114.6 0.7 convolution_convert_fusion.2
  115.3 1.2 convolution_multiply_fusion
  116.5 0.2 fusion.78
  116.7 1.7 convolution_convert_fusion.3
  118.4 3.2 %fusion.15 = bf16[32,32,512]{2,0,1:T(8,128)(2,1)} fusion(bf16[32,32,512]{2,1,0:T(8,128)(2,1)} %bitcast.173, f32[32,32]{1,0:T(8,128)S(1)} %fusion.78, f32[32,32,32]{1,2,0:T(8,128)S(1)} %convolution_multiply_fusion, pred[32,32]{0,1:T(8,128)(4,1)S(1)} %iota_compare_fusion.2), kind=kOutput, calls=%fused_computation.37 | convolution fusion | flops 34243616 | bytes 2233344 | tf_op jit(solution)/shard_map/nab,bnc->anc/dot_general | solution.py:108
  121.6 1.9 copy.93
  123.5 1.7 fusion.8
  125.2 3.7 %all-to-all-start.1 = ((bf16[32,32,512]{2,1,0:T(8,128)(2,1)}), bf16[32,32,512]{2,1,0:T(8,128)(2,1)S(1)}, u32[]{:S(2)}, u32[]{:S(2)}) async-start(bf16[32,32,512]{2,1,0:T(8,128)(2,1)} %bitcast.165), calls=%async_computation.1 | async-start | bytes 2097152 | tf_op jit(solution)/shard_map/all_to_all | solution.py:114
  128.9 44.8 %reduce-scatter.4.cloned.1.call-done = f32[96,512]{1,0:T(8,128)} async-done(((f32[1536,512]{1,0:T(8,128)}), f32[96,512]{1,0:T(8,128)}) %reduce-scatter.4.cloned.1.call-update) | async-done | bytes 196624 | tf_op jit(solution)/shard_map/reduce_scatter | solution.py:120
  173.7 22.2 %fusion = f32[16,512]{1,0:T(8,128)S(1)} fusion(f32[96,512]{1,0:T(8,128)} %reduce-scatter.4.cloned.1.call-done), kind=kCustom, calls=%all-reduce-scatter | all-reduce-scatter fusion | flops 65537 | bytes 229888
  195.9 2.7 %collective-permute-start.3 = (f32[16,512]{1,0:T(8,128)S(1)}, f32[16,512]{1,0:T(8,128)S(1)}, u32[]{:S(2)}, u32[]{:S(2)}) collective-permute-start(f32[16,512]{1,0:T(8,128)S(1)} %fusion), channel_id=1, source_target_pairs={{0,16},{16,32},{32,48},{48,64},{64,80},{80,96},{96,112},{1,17},{17... | collective-permute-start | bytes 98312
  198.6 2.8 %collective-permute-start.4 = (f32[12,512]{1,0:T(8,128)S(1)}, f32[12,512]{1,0:T(8,128)S(1)}, u32[]{:S(2)}, u32[]{:S(2)}) collective-permute-start(f32[12,512]{1,0:T(8,128)S(1)} %slice.121), channel_id=1, source_target_pairs={{0,32},{16,48},{32,64},{48,80},{64,96},{80,112},{1,33},{17,49},{33... | collective-permute-start | bytes 73736
  201.4 0.6 dynamic-slice.4
  202.6 1.0 copy.94
  203.7 0.3 concatenate.17
  204.0 0.1 reshape.150
  204.1 0.7 copy.102
  (43 shorter events, 0.4 us)
Async XLA Ops:
  7.2 106.4 %copy-start = (bf16[512,512]{1,0:T(8,128)(2,1)S(1)}, bf16[512,512]{1,0:T(8,128)(2,1)}, u32[]{:S(2)}) copy-start(bf16[512,512]{1,0:T(8,128)(2,1)} %param.14) | copy-start | bytes 1572868
  7.2 7.9 %copy-start.1 = (bf16[4,4,64,512]{3,2,1,0:T(8,128)(2,1)S(1)}, bf16[4,4,64,512]{3,2,1,0:T(8,128)(2,1)}, u32[]{:S(2)}) copy-start(bf16[4,4,64,512]{3,2,1,0:T(8,128)(2,1)} %param.9) | copy-start | bytes 3145732
  7.2 166.5 %reduce-scatter.4.cloned.1.call-start = ((), (), s32[]{:S(2)}) async-start(), calls=%async_computation.3 | async-start | bytes 3342336 | tf_op jit(solution)/shard_map/reduce_scatter | solution.py:120
  8.4 8.4 %collective-permute-start.1 = (bf16[4,1,64,512]{3,2,1,0:T(8,128)(2,1)S(1)}, bf16[4,1,64,512]{3,2,1,0:T(8,128)(2,1)S(1)}, u32[]{:S(2)}, u32[]{:S(2)}) collective-permute-start(bf16[4,1,64,512]{3,2,1,0:T(8,128)(2,1)S(1)} %get-tuple-element.23), channel_id=1, source_target_pairs={{1,0},{2,1},{3,2},{4,3},{5,4},{6,5},{7,6},{8,7},{9,8},{10,9},{11,1... | collective-permute-start | bytes 786440 | tf_op jit(solution)/shard_map/ppermute | solution.py:17
  9.7 7.1 %collective-permute-start = (bf16[4,1,64,512]{3,2,1,0:T(8,128)(2,1)S(1)}, bf16[4,1,64,512]{3,2,1,0:T(8,128)(2,1)S(1)}, u32[]{:S(2)}, u32[]{:S(2)}) collective-permute-start(bf16[4,1,64,512]{3,2,1,0:T(8,128)(2,1)S(1)} %get-tuple-element.22), channel_id=1, source_target_pairs={{0,1},{1,2},{2,3},{3,4},{4,5},{5,6},{6,7},{7,8},{8,9},{9,10},{10,1... | collective-permute-start | bytes 786440 | tf_op jit(solution)/shard_map/ppermute | solution.py:15
  16.8 2.4 %slice-start = ((s8[4718592]{0:T(1024)(128)(4,1)}), s8[4194304]{0:T(1024)(128)(4,1)S(1)}, s32[]{:S(2)}) async-start(s8[4718592]{0:T(1024)(128)(4,1)} %bitcast.152), calls=%async_computation.4 | async-start | bytes 8388608
  17.8 1.6 slice-start.1
  28.4 15.6 %collective-permute-start.2 = (bf16[2,4,64,512]{3,2,1,0:T(8,128)(2,1)}, bf16[2,4,64,512]{3,2,1,0:T(8,128)(2,1)S(1)}, u32[]{:S(2)}, u32[]{:S(2)}) collective-permute-start(bf16[2,4,64,512]{3,2,1,0:T(8,128)(2,1)} %bitcast.19), channel_id=1, source_target_pairs={{0,16},{16,32},{32,48},{48,64},{64,80},{80,96},{96,112},{1,17},{17... | collective-permute-start | bytes 1572872 | tf_op jit(solution)/shard_map/ppermute | solution.py:27
  36.0 3.2 %copy-start.8 = (bf16[512,1024]{1,0:T(8,128)(2,1)S(1)}, bf16[512,1024]{1,0:T(8,128)(2,1)}, u32[]{:S(2)}) copy-start(bf16[512,1024]{1,0:T(8,128)(2,1)} %copy.96) | copy-start | bytes 3145732
  36.0 3.2 %copy-start.9 = (bf16[512,1024]{1,0:T(8,128)(2,1)S(1)}, bf16[512,1024]{1,0:T(8,128)(2,1)}, u32[]{:S(2)}) copy-start(bf16[512,1024]{1,0:T(8,128)(2,1)} %copy.95) | copy-start | bytes 3145732
  39.2 4.9 %copy-start.6 = (bf16[4,4,64,512]{3,2,1,0:T(8,128)(2,1)S(1)}, bf16[4,4,64,512]{3,2,1,0:T(8,128)(2,1)}, u32[]{:S(2)}) copy-start(bf16[4,4,64,512]{3,2,1,0:T(8,128)(2,1)} %param.17) | copy-start | bytes 3145732
  48.5 3.4 %copy-start.7 = (bf16[4,4,64,512]{3,2,1,0:T(8,128)(2,1)S(1)}, bf16[4,4,64,512]{3,2,1,0:T(8,128)(2,1)}, u32[]{:S(2)}) copy-start(bf16[4,4,64,512]{3,2,1,0:T(8,128)(2,1)} %param.17) | copy-start | bytes 3145732
  56.4 2.2 %copy-start.3 = (f32[1,8,64,16,32]{2,4,3,1,0:T(8,128)S(1)}, f32[1,8,64,16,32]{2,4,3,1,0:T(8,128)}, u32[]{:S(2)}) copy-start(f32[1,8,64,16,32]{2,4,3,1,0:T(8,128)} %copy.100) | copy-start | bytes 3145732
  56.4 2.9 %copy-start.4 = (f32[1,8,64,16,32]{2,4,3,1,0:T(8,128)S(1)}, f32[1,8,64,16,32]{2,4,3,1,0:T(8,128)}, u32[]{:S(2)}) copy-start(f32[1,8,64,16,32]{2,4,3,1,0:T(8,128)} %convolution_bitcast_fusion) | copy-start | bytes 3145732
  82.2 1.4 copy-start.5
  82.4 1.9 copy-start.2
  87.1 22.5 %all-to-all-start = ((bf16[4,256,512]{2,0,1:T(4,128)(2,1)}), bf16[4,256,512]{2,0,1:T(4,128)(2,1)}, u32[]{:S(2)}, u32[]{:S(2)}) async-start(bf16[4,256,512]{2,0,1:T(4,128)(2,1)} %copy.85), calls=%async_computation | async-start | bytes 2097152 | tf_op jit(solution)/shard_map/all_to_all | solution.py:89
  109.6 3.7 %copy-start.11 = (f32[512]{0:T(512)S(1)}, f32[512]{0:T(512)}, u32[]{:S(2)}) copy-start(f32[512]{0:T(512)} %param.12) | copy-start | bytes 6148
  113.5 1.0 copy-start.13
  115.3 1.4 copy-start.14
  121.6 1.9 copy-start.10
  125.2 76.2 %copy-start.12 = (u32[128]{0:T(128)S(1)}, u32[128]{0:T(128)}, u32[]{:S(2)}) copy-start(u32[128]{0:T(128)} %constant.25) | copy-start | bytes 1540
  125.2 77.4 %all-to-all-start.1 = ((bf16[32,32,512]{2,1,0:T(8,128)(2,1)}), bf16[32,32,512]{2,1,0:T(8,128)(2,1)S(1)}, u32[]{:S(2)}, u32[]{:S(2)}) async-start(bf16[32,32,512]{2,1,0:T(8,128)(2,1)} %bitcast.165), calls=%async_computation.1 | async-start | bytes 2097152 | tf_op jit(solution)/shard_map/all_to_all | solution.py:114
  195.9 7.8 %collective-permute-start.3 = (f32[16,512]{1,0:T(8,128)S(1)}, f32[16,512]{1,0:T(8,128)S(1)}, u32[]{:S(2)}, u32[]{:S(2)}) collective-permute-start(f32[16,512]{1,0:T(8,128)S(1)} %fusion), channel_id=1, source_target_pairs={{0,16},{16,32},{32,48},{48,64},{64,80},{80,96},{96,112},{1,17},{17... | collective-permute-start | bytes 98312
  198.6 5.1 %collective-permute-start.4 = (f32[12,512]{1,0:T(8,128)S(1)}, f32[12,512]{1,0:T(8,128)S(1)}, u32[]{:S(2)}, u32[]{:S(2)}) collective-permute-start(f32[12,512]{1,0:T(8,128)S(1)} %slice.121), channel_id=1, source_target_pairs={{0,32},{16,48},{32,64},{48,80},{64,96},{80,112},{1,33},{17,49},{33... | collective-permute-start | bytes 73736
Sparse Core Ops, SparseCore 0:
  82.3 91.3 reduce-scatter.3

commit v2 on v0

v2 whole, which is shorter than its diff:
```python
import functools

import jax
import jax.numpy as jnp
from jax import lax
from jax.experimental import pallas as pl
from jax.experimental.pallas import tpu as pltpu
from jax.sharding import PartitionSpec as P

F32 = jnp.float32
BF16 = jnp.bfloat16
MESH = pl.DeviceIdType.MESH
CH = 512
TAPS = 3 * CH


def remote(src, dst, send_sem, recv_sem, device):
    return pltpu.make_async_remote_copy(
        src_ref=src,
        dst_ref=dst,
        send_sem=send_sem,
        recv_sem=recv_sem,
        device_id=device,
        device_id_type=MESH,
    )


def kernel(
    x_ref,
    wsp_ref,
    wt_ref,
    gain_ref,
    wq_ref,
    wk_ref,
    wv_ref,
    wo_ref,
    cot_ref,
    enc_ref,
    kg_ref,
    xpad,
    w2,
    wt,
    wq,
    wk,
    wv,
    wo,
    cot,
    cot_t,
    ext,
    ybuf,
    hid,
    hall,
    nrm,
    qb,
    kb,
    vb,
    sbuf,
    pbuf,
    ab,
    enc,
    part,
    a1,
    r1,
    a2,
    r2,
    a3,
    b4,
    a4,
    fin,
    w_sem,
    l_sem,
    row_send,
    row_recv,
    time_send,
    time_recv,
    hid_send,
    hid_recv,
    hid_own,
    enc_send,
    enc_recv,
    enc_own,
    s1_send,
    s1_recv,
    s2_send,
    s2_recv,
    s3_send,
    s3_recv,
    s4_send,
    s4_recv,
):
    t = lax.axis_index("tm")
    s = lax.axis_index("space")
    core = s % 2
    z = (s // 2) % 4
    y = s // 8

    own_x = pltpu.make_async_copy(x_ref, xpad.at[:, 64:320], l_sem.at[0])
    own_x.start()
    w_loads = []
    for dj in range(3):
        for di in range(3):
            load = pltpu.make_async_copy(
                wsp_ref.at[di, dj], w2.at[dj, di * CH : (di + 1) * CH], w_sem.at[3 * dj + di]
            )
            load.start()
            w_loads.append(load)
    loads = []
    for i, (src, dst) in enumerate(
        ((cot_ref, cot), (wt_ref, wt), (wq_ref, wq), (wk_ref, wk), (wv_ref, wv), (wo_ref, wo))
    ):
        load = pltpu.make_async_copy(src, dst, l_sem.at[1 + i])
        load.start()
        loads.append(load)

    below = {"space": (s + 1) % 16}
    above = {"space": (s + 15) % 16}
    z_peers = [{"space": y * 8 + ((z + o) % 4) * 2 + core} for o in range(1, 4)]
    y_peer = {"space": (1 - y) * 8 + z * 2 + core}
    core_peer = {"space": s + 1 - 2 * core}
    t_peers = [{"tm": (t + o) % 8} for o in range(1, 8)]

    barrier = pltpu.get_barrier_semaphore()
    for peer in [below, above, y_peer] + z_peers + t_peers:
        pl.semaphore_signal(barrier, inc=1, device_id=peer, device_id_type=MESH)
    pl.semaphore_wait(barrier, 13)

    to_below = remote(
        x_ref.at[:, 192:256], xpad.at[:, 0:64], row_send.at[0], row_recv.at[0], below
    )
    to_above = remote(
        x_ref.at[:, 0:64], xpad.at[:, 320:384], row_send.at[1], row_recv.at[1], above
    )
    to_below.start()
    to_above.start()

    column = lax.broadcasted_iota(jnp.int32, (64, 256), 0)

    def activate(chunks, place):
        def body(i, carry):
            frame, row = place(i)
            start = pl.multiple_of(i * 64, 64)
            to = pl.multiple_of(row * 64, 64)
            for half in range(2):
                lanes = slice(half * 256, half * 256 + 256)
                left = pltpu.roll(ybuf[0, pl.ds(start, 64), lanes], 1, 0)
                mid = ybuf[1, pl.ds(start, 64), lanes]
                right = pltpu.roll(ybuf[2, pl.ds(start, 64), lanes], 63, 0)
                v = mid + jnp.where(column == 0, 0.0, left) + jnp.where(column == 63, 0.0, right)
                ext[frame + 2, pl.ds(to, 64), lanes] = (v / (1.0 + jnp.exp(-v))).astype(BF16)
            return carry

        lax.fori_loop(0, chunks, body, 0)

    own_x.wait()
    for dj in range(3):
        for di in range(3):
            w_loads[3 * dj + di].wait()
        lhs = jnp.concatenate(
            [
                xpad[:, 64 * (1 + di) : 64 * (1 + di) + 128, :].reshape(512, CH)
                for di in range(3)
            ],
            axis=1,
        )
        ybuf[dj] = jnp.dot(lhs, w2[dj], preferred_element_type=F32)
    activate(8, lambda i: (i // 2, 1 + i % 2))

    loads[0].wait()
    for i in range(4):
        cot_t[:, 256 * i : 256 * i + 256] = cot[256 * i : 256 * i + 256, :].T

    to_below.wait()
    to_above.wait()

    @pl.when(s == 0)
    def _():
        xpad[:, 0:64, :] = jnp.zeros((4, 64, CH), BF16)

    @pl.when(s == 15)
    def _():
        xpad[:, 320:384, :] = jnp.zeros((4, 64, CH), BF16)

    def edges(first):
        for dj in range(3):
            lhs = jnp.concatenate(
                [
                    jnp.concatenate(
                        [
                            xpad[first : first + 2, 64 * di : 64 * di + 64, :],
                            xpad[first : first + 2, 64 * (3 + di) : 64 * (3 + di) + 64, :],
                        ],
                        axis=1,
                    ).reshape(256, CH)
                    for di in range(3)
                ],
                axis=1,
            )
            ybuf[dj, 0:256] = jnp.dot(lhs, w2[dj], preferred_element_type=F32)
        activate(4, lambda i: (first + i // 2, 3 * (i % 2)))

    edges(2)
    later = remote(
        ext.at[4:6], ext.at[0:2], time_send.at[0], time_recv.at[0], {"tm": (t + 1) % 8}
    )
    later.start()
    edges(0)

    loads[1].wait()

    def hidden(first):
        lhs = jnp.concatenate(
            [ext[first + 2 - k : first + 4 - k].reshape(512, CH) for k in range(3)], axis=1
        )
        temporal = jnp.dot(lhs, wt[...], preferred_element_type=F32)
        value = xpad[first : first + 2, 64:320, :].reshape(512, CH).astype(F32) + temporal
        value = value.astype(BF16)
        for f in range(2):
            hid[:, :, first + f] = value[256 * f : 256 * f + 256].reshape(8, 2, 16, CH)

    def hid_copies(first, g):
        pair = first // 2
        here = pl.ds(t * 4 + first, 2)
        copies = []
        for o in range(1, 8):
            copies.append(
                remote(
                    hid.at[(t + o) % 8, g, first : first + 2],
                    hall.at[g, here],
                    hid_send.at[pair, g, o - 1],
                    hid_recv.at[pair, g, o - 1],
                    t_peers[o - 1],
                )
            )
        own = pltpu.make_async_copy(
            hid.at[t, g, first : first + 2], hall.at[g, here], hid_own.at[pair, g]
        )
        return copies, own

    def send_hidden(first):
        started = []
        for g in range(2):
            copies, own = hid_copies(first, g)
            for copy in copies:
                copy.start()
            own.start()
            started.append((copies, own))
        return started

    hidden(2)
    hid_late = send_hidden(2)

    def tap(k):
        shifted = ext[2 - k : 6 - k].reshape(1024, CH)
        grad = jnp.dot(cot_t[...], shifted, preferred_element_type=F32).astype(BF16)
        part[:, :, :, k * CH : (k + 1) * CH] = grad.reshape(8, 2, 32, CH)

    tap(0)
    stage1 = [
        remote(
            part.at[:, 1 - core, :, lanes],
            a1.at[:, :, lanes],
            s1_send.at[i],
            s1_recv.at[i],
            core_peer,
        )
        for i, lanes in enumerate((slice(0, CH), slice(CH, TAPS)))
    ]
    stage1[0].start()

    later.wait()

    @pl.when(t == 0)
    def _():
        ext[0:2] = jnp.zeros((2, 256, CH), BF16)

    hidden(0)
    hid_early = send_hidden(0)

    tap(1)
    tap(2)
    stage1[1].start()
    for copy in stage1:
        copy.wait()
    for i in range(8):
        r1[i // 4, i % 4] = (part[i, core].astype(F32) + a1[i].astype(F32)).astype(BF16)
    stage2 = [
        remote(
            r1.at[:, (z + o) % 4], a2.at[o - 1], s2_send.at[o - 1], s2_recv.at[o - 1], z_peers[o - 1]
        )
        for o in range(1, 4)
    ]
    for copy in stage2:
        copy.start()

    for load in loads[2:]:
        load.wait()

    scale = 1.0 / (CH**0.5)

    def project(g):
        for started in (hid_late, hid_early):
            copies, own = started[g]
            for copy in copies:
                copy.wait_recv()
            own.wait()
        def norm_rows(i, carry):
            wide = hall[g, pl.ds(i * 8, 8)].reshape(128, CH).astype(F32)
            inv = 1.0 / jnp.sqrt(jnp.mean(wide * wide, axis=1, keepdims=True) + 1e-06)
            rows = pl.ds(pl.multiple_of(i * 128, 128), 128)
            nrm[rows, :] = (wide * inv * gain_ref[...]).astype(BF16)
            return carry

        lax.fori_loop(0, 4, norm_rows, 0)
        for weight, out in ((wq, qb), (wk, kb), (wv, vb)):
            out[...] = jnp.dot(nrm[...], weight[...], preferred_element_type=F32).astype(BF16)

    def attend(g, tile):
        keys = 256 * (tile + 1)
        base = 256 * tile
        sbuf[:, :keys] = lax.dot_general(
            qb[base : base + 256, :],
            kb[:keys, :],
            (((1,), (1,)), ((), ())),
            preferred_element_type=F32,
        )

        def soft(i, carry):
            rows = pl.ds(pl.multiple_of(i * 64, 64), 64)
            scores = sbuf[rows, :keys] * scale
            row = lax.broadcasted_iota(jnp.int32, (64, keys), 0) + (base + i * 64)
            col = lax.broadcasted_iota(jnp.int32, (64, keys), 1)
            allowed = (((row ^ col) & 15) == 0) & (col <= row)
            scores = jnp.where(allowed, scores, -1e30)
            expon = jnp.where(
                allowed, jnp.exp(scores - jnp.max(scores, axis=1, keepdims=True)), 0.0
            )
            total = jnp.sum(expon, axis=1, keepdims=True)
            pbuf[rows, :keys] = (expon * (1.0 / total)).astype(BF16)
            return carry

        lax.fori_loop(0, 4, soft, 0)
        ab[...] = jnp.dot(pbuf[:, :keys], vb[:keys, :], preferred_element_type=F32).astype(BF16)
        back = jnp.dot(ab[...], wo[...], preferred_element_type=F32)
        frames = slice(16 * tile, 16 * tile + 16)
        wide = hall[g, frames].reshape(256, CH).astype(F32)
        enc[g, frames] = (wide + back).astype(BF16).reshape(16, 16, CH)

    def enc_copy(g, o):
        p = (t + o) % 8
        return remote(
            enc.at[g, pl.ds(p * 4, 4)],
            enc_ref.at[:, t, g],
            enc_send.at[g, o],
            enc_recv.at[g, o],
            {"tm": p},
        )

    def enc_local(g):
        return pltpu.make_async_copy(
            enc.at[g, pl.ds(t * 4, 4)], enc_ref.at[:, t, g], enc_own.at[g]
        )

    def send_encoded(g, tile):
        for o in range(8):
            p = (t + o) % 8

            @pl.when(p // 4 == tile)
            def _():
                if o == 0:
                    enc_local(g).start()
                else:
                    enc_copy(g, o).start()

    project(0)
    attend(0, 0)
    send_encoded(0, 0)
    for copy in stage2:
        copy.wait()
    for i in range(2):
        r2[i] = (
            r1[i, z].astype(F32)
            + a2[0, i].astype(F32)
            + a2[1, i].astype(F32)
            + a2[2, i].astype(F32)
        ).astype(BF16)
    stage3 = remote(r2.at[1 - y], a3, s3_send.at[0], s3_recv.at[0], y_peer)
    stage3.start()
    attend(0, 1)
    send_encoded(0, 1)

    project(1)
    stage3.wait()
    for k in range(3):
        for q in range(4):
            lanes = slice(k * CH + q * 128, k * CH + q * 128 + 128)
            b4[q, k] = (r2[y, :, lanes].astype(F32) + a3[:, lanes].astype(F32)).astype(BF16)
    stage4 = [
        remote(
            b4.at[((t + o) % 8) // 2],
            a4.at[o - 1],
            s4_send.at[o - 1],
            s4_recv.at[o - 1],
            t_peers[o - 1],
        )
        for o in range(1, 8)
    ]
    for copy in stage4:
        copy.start()
    attend(1, 0)
    send_encoded(1, 0)
    attend(1, 1)
    send_encoded(1, 1)

    for copy in stage4:
        copy.wait()
    for k in range(3):
        total = b4[t // 2, k].astype(F32)
        for o in range(7):
            total = total + a4[o, k].astype(F32)
        fin[k] = total.T
    kg_ref[...] = fin[:, pl.ds(pl.multiple_of((t % 2) * 64, 64), 64), :]

    for started in hid_late + hid_early:
        for copy in started[0]:
            copy.wait_send()
    for g in range(2):
        enc_local(g).wait()
        for o in range(1, 8):
            enc_copy(g, o).wait()


def on_device(
    frames_in,
    spatial_kernel,
    temporal_kernel,
    norm_gain,
    query_weight,
    key_weight,
    value_weight,
    out_weight,
    cotangent,
):
    frames, rows, cols, chans = frames_in.shape
    anywhere = pl.BlockSpec(memory_space=pl.ANY)
    vmem = pl.BlockSpec(memory_space=pltpu.VMEM)
    dma = pltpu.SemaphoreType.DMA
    square = pltpu.VMEM((CH, CH), BF16)
    encoded, grad = pl.pallas_call(
        kernel,
        name="block",
        out_shape=(
            jax.ShapeDtypeStruct((4, 8, 2, 16, CH), BF16),
            jax.ShapeDtypeStruct((3, 64, 32), F32),
        ),
        in_specs=[anywhere] * 3 + [vmem] + [anywhere] * 5,
        out_specs=(anywhere, vmem),
        scratch_shapes=[
            pltpu.VMEM((4, 384, CH), BF16),
            pltpu.VMEM((3, TAPS, CH), BF16),
            pltpu.VMEM((TAPS, CH), BF16),
            square,
            square,
            square,
            square,
            pltpu.VMEM((1024, CH), BF16),
            pltpu.VMEM((CH, 1024), BF16),
            pltpu.VMEM((6, 256, CH), BF16),
            pltpu.VMEM((3, 512, CH), F32),
            pltpu.VMEM((8, 2, 4, 16, CH), BF16),
            pltpu.VMEM((2, 32, 16, CH), BF16),
            square,
            square,
            square,
            square,
            pltpu.VMEM((256, 512), F32),
            pltpu.VMEM((256, 512), BF16),
            pltpu.VMEM((256, CH), BF16),
            pltpu.VMEM((2, 32, 16, CH), BF16),
            pltpu.VMEM((8, 2, 32, TAPS), BF16),
            pltpu.VMEM((8, 32, TAPS), BF16),
            pltpu.VMEM((2, 4, 32, TAPS), BF16),
            pltpu.VMEM((3, 2, 32, TAPS), BF16),
            pltpu.VMEM((2, 32, TAPS), BF16),
            pltpu.VMEM((32, TAPS), BF16),
            pltpu.VMEM((4, 3, 32, 128), BF16),
            pltpu.VMEM((7, 3, 32, 128), BF16),
            pltpu.VMEM((3, 128, 32), F32),
            dma((9,)),
            dma((7,)),
            dma((2,)),
            dma((2,)),
            dma((1,)),
            dma((1,)),
            dma((2, 2, 7)),
            dma((2, 2, 7)),
            dma((2, 2)),
            dma((2, 8)),
            dma((2, 8)),
            dma((2,)),
            dma((2,)),
            dma((2,)),
            dma((3,)),
            dma((3,)),
            dma((1,)),
            dma((1,)),
            dma((7,)),
            dma((7,)),
        ],
        compiler_params=pltpu.CompilerParams(
            collective_id=0, has_side_effects=True, vmem_limit_bytes=60 * 1024 * 1024
        ),
    )(
        frames_in.reshape(frames, rows * cols, chans),
        spatial_kernel,
        temporal_kernel.reshape(3 * chans, chans),
        norm_gain.reshape(1, chans),
        query_weight,
        key_weight,
        value_weight,
        out_weight,
        cotangent.reshape(-1, chans),
    )
    return (encoded.reshape(frames, rows, cols, chans), grad)


def solution(mesh):
    tile = P("tm", "space", None, None)
    in_specs = (tile, P(), P(), P(), P(), P(), P(), P(), tile)
    out_specs = (tile, P(None, "tm", "space"))
    return jax.shard_map(
        on_device, mesh=mesh, in_specs=in_specs, out_specs=out_specs, check_vma=False
    )
```

time: 466 us -> 76.4 us (0.16)
  waiting for transfers between devices: 368 us -> 0 us
  Pallas kernels: 0 us -> 70.8 us
  matrix products: 39.1 us -> 0 us
  local copies, waits for them, and re-layouts: 30.6 us -> 3.89 us
  between operations: 14.7 us -> 0.64 us
  starting transfers between devices: 6.72 us -> 0 us
  other arithmetic: 5.3 us -> 0 us
    unnamed x6 -> x0, waiting for transfers between devices: 185 us -> none
    all_gather x2 -> x0, waiting for transfers between devices: 173 us -> none  [the longest x1 89.4 us: on_device(): key_piece = lax.all_gather(key, 'tm', axis=0, tiled=True)]
    pallas_call x0 -> x1, Pallas kernels: none -> 70.8 us  [on_device(): pl.pallas_call(kernel, name='block', out_shape=(jax.ShapeDtypeStruct((4,...]
    dot_general x21 -> x0, matrix products: 39.1 us -> none  [the longest x1 9 us: on_device(): new_acc = jnp.einsum('abn,bnc->anc', expon, value_piece.astype(jnp.float32))]
    unnamed x32 -> x2, local copies, waits for them, and re-layouts: 22.8 us -> 3.89 us
    ppermute x3 -> x0, waiting for transfers between devices: 9.93 us -> none  [the longest x1 7.66 us: from_behind(): lax.ppermute(value, axis, [(source, source + steps) for source in range(f...]
    ppermute x3 -> x0, starting transfers between devices: 6.16 us -> none  [the longest x1 3.43 us: from_behind(): lax.ppermute(value, axis, [(source, source + steps) for source in range(f...]
    another operation x1 -> x0, local copies, waits for them, and re-layouts: 5.09 us -> none  [on_device(): partial_grad = jnp.stack(grads, axis=0)]
  transfers between devices with their start and end apart: 7 -> 0, of which waited for: 6 -> 0; matrix products, arithmetic and copies ran while one was open for 6% -> 0% of each run, Pallas kernels for 0% -> 0%
where the time goes in v2:
time: 76.4 us; the launch traced here: 75.3 us
  Pallas kernels  70.8 us (93%)
  local copies, waits for them, and re-layouts  3.89 us (5%)
    pallas_call x1, Pallas kernels, on_device(): pl.pallas_call(kernel, name='block', out_shape=(jax.ShapeDtypeStruct((4,...  70.8 us
    unnamed x2, local copies, waits for them, and re-layouts  3.89 us

profile of v2, /device:TPU:0, one launch (start us, length us, event | category | flops | bytes accessed | tf_op | source)
XLA Modules:
  0.0 75.3 jit_solution(8709437356525176884)
XLA Ops:
  0.6 70.8 %block.1 = (bf16[4,8,2,16,512]{4,3,2,1,0:T(8,128)(2,1)}, f32[3,64,32]{2,1,0:T(8,128)}) custom-call(bf16[4,256,512]{2,1,0:T(8,128)(2,1)} %bitcast.7, bf16[3,3,512,512]{3,2,1,0:T(8,128)(2,1)} %wsp_ref.1, bf16[1536,512]{1,0:T(8,128)(2,1)} %bitcast.5, f32[1,512]{1,0:T(1,128)} %bitcast.9, bf16[512,512]{1,0:T(8,128)(2,1)} %wq_ref.1, bf16[512,512]{1,0:T(8,128)(2,1)} %wk_ref.1, ...), custom_call_target="tpu_custom_call" | custom-call | tf_op jit(solution)/shard_map/block/pallas_call | solution.py:448
  71.4 1.6 %copy.11 = f32[3,64,32]{1,2,0:T(8,128)} copy(f32[3,64,32]{2,1,0:T(8,128)} %get-tuple-element.7) | data formatting | bytes 49152
  73.0 2.3 %copy.13 = bf16[4,4,64,512]{3,2,1,0:T(8,128)(2,1)} copy(bf16[4,4,64,512]{3,2,1,0:T(8,128)(2,1)} %bitcast.6) | data formatting | bytes 2097152

commit v3 on v2

--- a/solution.py
+++ b/solution.py
@@ -66,7 +66,6 @@
     a3,
     b4,
     a4,
-    fin,
     w_sem,
     l_sem,
     row_send,
@@ -94,6 +93,17 @@
     z = (s // 2) % 4
     y = s // 8
 
+    below = {"space": (s + 1) % 16}
+    above = {"space": (s + 15) % 16}
+    z_peers = [{"space": y * 8 + ((z + o) % 4) * 2 + core} for o in range(1, 4)]
+    y_peer = {"space": (1 - y) * 8 + z * 2 + core}
+    core_peer = {"space": s + 1 - 2 * core}
+    t_peers = [{"tm": (t + o) % 8} for o in range(1, 8)]
+
+    barrier = pltpu.get_barrier_semaphore()
+    for peer in [below, above, y_peer] + z_peers + t_peers:
+        pl.semaphore_signal(barrier, inc=1, device_id=peer, device_id_type=MESH)
+
     own_x = pltpu.make_async_copy(x_ref, xpad.at[:, 64:320], l_sem.at[0])
     own_x.start()
     w_loads = []
@@ -108,34 +118,32 @@
     for i, (src, dst) in enumerate(
         ((cot_ref, cot), (wt_ref, wt), (wq_ref, wq), (wk_ref, wk), (wv_ref, wv), (wo_ref, wo))
     ):
-        load = pltpu.make_async_copy(src, dst, l_sem.at[1 + i])
-        load.start()
-        loads.append(load)
-
-    below = {"space": (s + 1) % 16}
-    above = {"space": (s + 15) % 16}
-    z_peers = [{"space": y * 8 + ((z + o) % 4) * 2 + core} for o in range(1, 4)]
-    y_peer = {"space": (1 - y) * 8 + z * 2 + core}
-    core_peer = {"space": s + 1 - 2 * core}
-    t_peers = [{"tm": (t + o) % 8} for o in range(1, 8)]
-
-    barrier = pltpu.get_barrier_semaphore()
-    for peer in [below, above, y_peer] + z_peers + t_peers:
-        pl.semaphore_signal(barrier, inc=1, device_id=peer, device_id_type=MESH)
-    pl.semaphore_wait(barrier, 13)
-
-    to_below = remote(
-        x_ref.at[:, 192:256], xpad.at[:, 0:64], row_send.at[0], row_recv.at[0], below
-    )
-    to_above = remote(
-        x_ref.at[:, 0:64], xpad.at[:, 320:384], row_send.at[1], row_recv.at[1], above
-    )
-    to_below.start()
-    to_above.start()
+        loads.append(pltpu.make_async_copy(src, dst, l_sem.at[1 + i]))
+
+    rows_in = {}
+    for first in (2, 0):
+        frames = slice(first, first + 2)
+        pair = first // 2
+        rows_in[first] = [
+            remote(
+                x_ref.at[frames, 192:256],
+                xpad.at[frames, 0:64],
+                row_send.at[pair, 0],
+                row_recv.at[pair, 0],
+                below,
+            ),
+            remote(
+                x_ref.at[frames, 0:64],
+                xpad.at[frames, 320:384],
+                row_send.at[pair, 1],
+                row_recv.at[pair, 1],
+                above,
+            ),
+        ]
 
     column = lax.broadcasted_iota(jnp.int32, (64, 256), 0)
 
-    def activate(chunks, place):
+    def activate(place):
         def body(i, carry):
             frame, row = place(i)
             start = pl.multiple_of(i * 64, 64)
@@ -149,38 +157,39 @@
                 ext[frame + 2, pl.ds(to, 64), lanes] = (v / (1.0 + jnp.exp(-v))).astype(BF16)
             return carry
 
-        lax.fori_loop(0, chunks, body, 0)
-
-    own_x.wait()
-    for dj in range(3):
-        for di in range(3):
-            w_loads[3 * dj + di].wait()
-        lhs = jnp.concatenate(
-            [
-                xpad[:, 64 * (1 + di) : 64 * (1 + di) + 128, :].reshape(512, CH)
-                for di in range(3)
-            ],
-            axis=1,
-        )
-        ybuf[dj] = jnp.dot(lhs, w2[dj], preferred_element_type=F32)
-    activate(8, lambda i: (i // 2, 1 + i % 2))
-
-    loads[0].wait()
-    for i in range(4):
-        cot_t[:, 256 * i : 256 * i + 256] = cot[256 * i : 256 * i + 256, :].T
-
-    to_below.wait()
-    to_above.wait()
-
-    @pl.when(s == 0)
-    def _():
-        xpad[:, 0:64, :] = jnp.zeros((4, 64, CH), BF16)
-
-    @pl.when(s == 15)
-    def _():
-        xpad[:, 320:384, :] = jnp.zeros((4, 64, CH), BF16)
+        lax.fori_loop(0, 4, body, 0)
+
+    def middle(first, weights=()):
+        for dj in range(3):
+            for load in weights[3 * dj : 3 * dj + 3]:
+                load.wait()
+            lhs = jnp.concatenate(
+                [
+                    xpad[first : first + 2, 64 * (1 + di) : 64 * (1 + di) + 128, :].reshape(256, CH)
+                    for di in range(3)
+                ],
+                axis=1,
+            )
+            ybuf[dj] = jnp.dot(lhs, w2[dj], preferred_element_type=F32)
+        activate(lambda i: (first + i // 2, 1 + i % 2))
 
     def edges(first):
+        @pl.when(s > 0)
+        def _():
+            rows_in[first][0].wait_recv()
+
+        @pl.when(s < 15)
+        def _():
+            rows_in[first][1].wait_recv()
+
+        @pl.when(s == 0)
+        def _():
+            xpad[first : first + 2, 0:64, :] = jnp.zeros((2, 64, CH), BF16)
+
+        @pl.when(s == 15)
+        def _():
+            xpad[first : first + 2, 320:384, :] = jnp.zeros((2, 64, CH), BF16)
+
         for dj in range(3):
             lhs = jnp.concatenate(
                 [
@@ -195,14 +204,45 @@
                 ],
                 axis=1,
             )
-            ybuf[dj, 0:256] = jnp.dot(lhs, w2[dj], preferred_element_type=F32)
-        activate(4, lambda i: (first + i // 2, 3 * (i % 2)))
-
+            ybuf[dj] = jnp.dot(lhs, w2[dj], preferred_element_type=F32)
+        activate(lambda i: (first + i // 2, 3 * (i % 2)))
+
+    later = [
+        remote(
+            ext.at[4:6, rows],
+            ext.at[0:2, rows],
+            time_send.at[i],
+            time_recv.at[i],
+            {"tm": (t + 1) % 8},
+        )
+        for i, rows in enumerate((slice(64, 192), slice(0, 64), slice(192, 256)))
+    ]
+
+    pl.semaphore_wait(barrier, 13)
+    @pl.when(s < 15)
+    def _():
+        rows_in[2][0].start()
+        rows_in[0][0].start()
+
+    @pl.when(s > 0)
+    def _():
+        rows_in[2][1].start()
+        rows_in[0][1].start()
+
+    own_x.wait()
+    def send_later(pieces):
+        @pl.when(t < 7)
+        def _():
+            for copy in pieces:
+                copy.start()
+
+    middle(2, w_loads)
+    send_later(later[:1])
+    for load in loads:
+        load.start()
     edges(2)
-    later = remote(
-        ext.at[4:6], ext.at[0:2], time_send.at[0], time_recv.at[0], {"tm": (t + 1) % 8}
-    )
-    later.start()
+    send_later(later[1:])
+    middle(0)
     edges(0)
 
     loads[1].wait()
@@ -219,35 +259,37 @@
 
     def hid_copies(first, g):
         pair = first // 2
-        here = pl.ds(t * 4 + first, 2)
         copies = []
         for o in range(1, 8):
             copies.append(
                 remote(
                     hid.at[(t + o) % 8, g, first : first + 2],
-                    hall.at[g, here],
+                    hall.at[g, t, first : first + 2],
                     hid_send.at[pair, g, o - 1],
                     hid_recv.at[pair, g, o - 1],
                     t_peers[o - 1],
                 )
             )
         own = pltpu.make_async_copy(
-            hid.at[t, g, first : first + 2], hall.at[g, here], hid_own.at[pair, g]
+            hid.at[t, g, first : first + 2], hall.at[g, t, first : first + 2], hid_own.at[pair, g]
         )
         return copies, own
 
-    def send_hidden(first):
-        started = []
-        for g in range(2):
-            copies, own = hid_copies(first, g)
-            for copy in copies:
-                copy.start()
-            own.start()
-            started.append((copies, own))
-        return started
+    hid_late = [hid_copies(2, g) for g in range(2)]
+    hid_early = [hid_copies(0, g) for g in range(2)]
+
+    def send_hidden(exchange):
+        copies, own = exchange
+        for copy in copies:
+            copy.start()
+        own.start()
 
     hidden(2)
-    hid_late = send_hidden(2)
+    send_hidden(hid_late[0])
+
+    loads[0].wait()
+    for i in range(4):
+        cot_t[:, 256 * i : 256 * i + 256] = cot[256 * i : 256 * i + 256, :].T
 
     def tap(k):
         shifted = ext[2 - k : 6 - k].reshape(1024, CH)
@@ -267,59 +309,52 @@
     ]
     stage1[0].start()
 
-    later.wait()
+    @pl.when(t > 0)
+    def _():
+        for copy in later:
+            copy.wait_recv()
 
     @pl.when(t == 0)
     def _():
         ext[0:2] = jnp.zeros((2, 256, CH), BF16)
 
     hidden(0)
-    hid_early = send_hidden(0)
+    send_hidden(hid_early[0])
+    send_hidden(hid_late[1])
+    send_hidden(hid_early[1])
 
     tap(1)
     tap(2)
     stage1[1].start()
-    for copy in stage1:
-        copy.wait()
-    for i in range(8):
-        r1[i // 4, i % 4] = (part[i, core].astype(F32) + a1[i].astype(F32)).astype(BF16)
-    stage2 = [
-        remote(
-            r1.at[:, (z + o) % 4], a2.at[o - 1], s2_send.at[o - 1], s2_recv.at[o - 1], z_peers[o - 1]
-        )
-        for o in range(1, 4)
-    ]
-    for copy in stage2:
-        copy.start()
+    scale = 1.0 / (CH**0.5)
 
     for load in loads[2:]:
         load.wait()
 
-    scale = 1.0 / (CH**0.5)
-
-    def project(g):
-        for started in (hid_late, hid_early):
-            copies, own = started[g]
-            for copy in copies:
-                copy.wait_recv()
-            own.wait()
+    def project(started, first, g):
+        copies, own = started[g]
+        for copy in copies:
+            copy.wait_recv()
+        own.wait()
+
         def norm_rows(i, carry):
-            wide = hall[g, pl.ds(i * 8, 8)].reshape(128, CH).astype(F32)
+            wide = hall[g, pl.ds(i * 4, 4), first : first + 2].reshape(128, CH).astype(F32)
             inv = 1.0 / jnp.sqrt(jnp.mean(wide * wide, axis=1, keepdims=True) + 1e-06)
             rows = pl.ds(pl.multiple_of(i * 128, 128), 128)
             nrm[rows, :] = (wide * inv * gain_ref[...]).astype(BF16)
             return carry
 
-        lax.fori_loop(0, 4, norm_rows, 0)
+        lax.fori_loop(0, 2, norm_rows, 0)
         for weight, out in ((wq, qb), (wk, kb), (wv, vb)):
-            out[...] = jnp.dot(nrm[...], weight[...], preferred_element_type=F32).astype(BF16)
+            value = jnp.dot(nrm[...], weight[...], preferred_element_type=F32).astype(BF16)
+            out[g, :, first : first + 2] = value.reshape(8, 2, 16, CH)
 
     def attend(g, tile):
         keys = 256 * (tile + 1)
         base = 256 * tile
         sbuf[:, :keys] = lax.dot_general(
-            qb[base : base + 256, :],
-            kb[:keys, :],
+            qb[g, 4 * tile : 4 * tile + 4].reshape(256, CH),
+            kb[g, : 4 * tile + 4].reshape(keys, CH),
             (((1,), (1,)), ((), ())),
             preferred_element_type=F32,
         )
@@ -339,10 +374,11 @@
             return carry
 
         lax.fori_loop(0, 4, soft, 0)
-        ab[...] = jnp.dot(pbuf[:, :keys], vb[:keys, :], preferred_element_type=F32).astype(BF16)
+        values = vb[g, : 4 * tile + 4].reshape(keys, CH)
+        ab[...] = jnp.dot(pbuf[:, :keys], values, preferred_element_type=F32).astype(BF16)
         back = jnp.dot(ab[...], wo[...], preferred_element_type=F32)
         frames = slice(16 * tile, 16 * tile + 16)
-        wide = hall[g, frames].reshape(256, CH).astype(F32)
+        wide = hall[g, 4 * tile : 4 * tile + 4].reshape(256, CH).astype(F32)
         enc[g, frames] = (wide + back).astype(BF16).reshape(16, 16, CH)
 
     def enc_copy(g, o):
@@ -371,9 +407,31 @@
                 else:
                     enc_copy(g, o).start()
 
-    project(0)
+    project(hid_late, 2, 0)
+    for copy in stage1:
+        copy.wait()
+    for i in range(8):
+        r1[i // 4, i % 4] = (part[i, core].astype(F32) + a1[i].astype(F32)).astype(BF16)
+    stage2 = [
+        remote(
+            r1.at[:, (z + o) % 4], a2.at[o - 1], s2_send.at[o - 1], s2_recv.at[o - 1], z_peers[o - 1]
+        )
+        for o in range(1, 4)
+    ]
+    for copy in stage2:
+        copy.start()
+
+    project(hid_early, 0, 0)
     attend(0, 0)
     send_encoded(0, 0)
+    attend(0, 1)
+    send_encoded(0, 1)
+    project(hid_late, 2, 1)
+    project(hid_early, 0, 1)
+    attend(1, 0)
+    send_encoded(1, 0)
+    attend(1, 1)
+    send_encoded(1, 1)
     for copy in stage2:
         copy.wait()
     for i in range(2):
@@ -385,10 +443,6 @@
         ).astype(BF16)
     stage3 = remote(r2.at[1 - y], a3, s3_send.at[0], s3_recv.at[0], y_peer)
     stage3.start()
-    attend(0, 1)
-    send_encoded(0, 1)
-
-    project(1)
     stage3.wait()
     for k in range(3):
         for q in range(4):
@@ -406,10 +460,6 @@
     ]
     for copy in stage4:
         copy.start()
-    attend(1, 0)
-    send_encoded(1, 0)
-    attend(1, 1)
-    send_encoded(1, 1)
 
     for copy in stage4:
         copy.wait()
@@ -417,8 +467,22 @@
         total = b4[t // 2, k].astype(F32)
         for o in range(7):
             total = total + a4[o, k].astype(F32)
-        fin[k] = total.T
-    kg_ref[...] = fin[:, pl.ds(pl.multiple_of((t % 2) * 64, 64), 64), :]
+        kg_ref[k] = jnp.where(t % 2 == 0, total[:, :64], total[:, 64:])
+
+    @pl.when(s < 15)
+    def _():
+        rows_in[2][0].wait_send()
+        rows_in[0][0].wait_send()
+
+    @pl.when(s > 0)
+    def _():
+        rows_in[2][1].wait_send()
+        rows_in[0][1].wait_send()
+
+    @pl.when(t < 7)
+    def _():
+        for copy in later:
+            copy.wait_send()
 
     for started in hid_late + hid_early:
         for copy in started[0]:
@@ -427,6 +491,20 @@
         enc_local(g).wait()
         for o in range(1, 8):
             enc_copy(g, o).wait()
+
+
+def place(enc_ref, kg_ref, enc_out, kg_out, held, held_grad, in_sem, out_sem):
+    pieces = [(enc_ref.at[f], held.at[f], enc_out.at[f]) for f in range(4)]
+    pieces.append((kg_ref, held_grad, kg_out))
+    loads = [pltpu.make_async_copy(a, b, in_sem.at[i]) for i, (a, b, _) in enumerate(pieces)]
+    stores = [pltpu.make_async_copy(b, c, out_sem.at[i]) for i, (_, b, c) in enumerate(pieces)]
+    for load in loads:
+        load.start()
+    for load, store in zip(loads, stores):
+        load.wait()
+        store.start()
+    for store in stores:
+        store.wait()
 
 
 def on_device(
@@ -450,7 +528,7 @@
         name="block",
         out_shape=(
             jax.ShapeDtypeStruct((4, 8, 2, 16, CH), BF16),
-            jax.ShapeDtypeStruct((3, 64, 32), F32),
+            jax.ShapeDtypeStruct((3, 32, 64), F32),
         ),
         in_specs=[anywhere] * 3 + [vmem] + [anywhere] * 5,
         out_specs=(anywhere, vmem),
@@ -465,13 +543,13 @@
             pltpu.VMEM((1024, CH), BF16),
             pltpu.VMEM((CH, 1024), BF16),
             pltpu.VMEM((6, 256, CH), BF16),
-            pltpu.VMEM((3, 512, CH), F32),
+            pltpu.VMEM((3, 256, CH), F32),
             pltpu.VMEM((8, 2, 4, 16, CH), BF16),
-            pltpu.VMEM((2, 32, 16, CH), BF16),
-            square,
-            square,
-            square,
-            square,
+            pltpu.VMEM((2, 8, 4, 16, CH), BF16),
+            pltpu.VMEM((256, CH), BF16),
+            pltpu.VMEM((2, 8, 4, 16, CH), BF16),
+            pltpu.VMEM((2, 8, 4, 16, CH), BF16),
+            pltpu.VMEM((2, 8, 4, 16, CH), BF16),
             pltpu.VMEM((256, 512), F32),
             pltpu.VMEM((256, 512), BF16),
             pltpu.VMEM((256, CH), BF16),
@@ -484,13 +562,12 @@
             pltpu.VMEM((32, TAPS), BF16),
             pltpu.VMEM((4, 3, 32, 128), BF16),
             pltpu.VMEM((7, 3, 32, 128), BF16),
-            pltpu.VMEM((3, 128, 32), F32),
             dma((9,)),
             dma((7,)),
-            dma((2,)),
-            dma((2,)),
-            dma((1,)),
-            dma((1,)),
+            dma((2, 2)),
+            dma((2, 2)),
+            dma((3,)),
+            dma((3,)),
             dma((2, 2, 7)),
             dma((2, 2, 7)),
             dma((2, 2)),
@@ -520,7 +597,24 @@
         out_weight,
         cotangent.reshape(-1, chans),
     )
-    return (encoded.reshape(frames, rows, cols, chans), grad)
+    encoded, grad = pl.pallas_call(
+        place,
+        name="place",
+        out_shape=(
+            jax.ShapeDtypeStruct((frames, rows * cols, chans), BF16),
+            jax.ShapeDtypeStruct((3, 32, 64), F32),
+        ),
+        in_specs=[anywhere] * 2,
+        out_specs=(anywhere, anywhere),
+        scratch_shapes=[
+            pltpu.VMEM((4, 256, CH), BF16),
+            pltpu.VMEM((3, 32, 64), F32),
+            dma((5,)),
+            dma((5,)),
+        ],
+        compiler_params=pltpu.CompilerParams(vmem_limit_bytes=60 * 1024 * 1024),
+    )(encoded.reshape(frames, rows * cols, chans), grad)
+    return (encoded.reshape(frames, rows, cols, chans), grad.transpose(0, 2, 1))
 
 
 def solution(mesh):

time: 76.4 us -> 59.4 us (0.78); the launches traced: 75.3 us -> 59.3 us
  Pallas kernels: 70.8 us -> 58.6 us
  local copies, waits for them, and re-layouts: 3.89 us -> 0 us
    pallas_call x1, Pallas kernels: 70.8 us -> 56.6 us  [on_device(): pl.pallas_call(kernel, name='block', out_shape=(jax.ShapeDtypeStruct((4,...]
    unnamed x2 -> x0, local copies, waits for them, and re-layouts: 3.89 us -> none
    pallas_call x0 -> x1, Pallas kernels: none -> 2 us  [on_device(): pl.pallas_call(place, name='place', out_shape=(jax.ShapeDtypeStruct((fram...]
where the time goes in v3:
time: 59.4 us; the launch traced here: 59.3 us
  Pallas kernels  58.6 us (99%)
  between operations  0.64 us (1%)
    pallas_call x1, Pallas kernels, on_device(): pl.pallas_call(kernel, name='block', out_shape=(jax.ShapeDtypeStruct((4,...  56.6 us
    pallas_call x1, Pallas kernels, on_device(): pl.pallas_call(place, name='place', out_shape=(jax.ShapeDtypeStruct((fram...  2 us

profile of v3, /device:TPU:0, one launch (start us, length us, event | category | flops | bytes accessed | tf_op | source)
XLA Modules:
  0.0 59.3 jit_solution(10305766623639918369)
XLA Ops:
  0.6 56.6 %block.1 = (bf16[4,8,2,16,512]{4,3,2,1,0:T(8,128)(2,1)}, f32[3,32,64]{2,1,0:T(8,128)}) custom-call(bf16[4,256,512]{2,1,0:T(8,128)(2,1)} %bitcast.9, bf16[3,3,512,512]{3,2,1,0:T(8,128)(2,1)} %wsp_ref.1, bf16[1536,512]{1,0:T(8,128)(2,1)} %bitcast.7, f32[1,512]{1,0:T(1,128)} %bitcast.11, bf16[512,512]{1,0:T(8,128)(2,1)} %wq_ref.1, bf16[512,512]{1,0:T(8,128)(2,1)} %wk_ref.1, ...), custom_call_target="tpu_custom_call" | custom-call | tf_op jit(solution)/shard_map/block/pallas_call | solution.py:526
  57.3 2.0 %place.1 = (bf16[4,256,512]{2,1,0:T(8,128)(2,1)}, f32[3,32,64]{2,1,0:T(8,128)}) custom-call(bf16[4,256,512]{2,1,0:T(8,128)(2,1)} %bitcast.8, f32[3,32,64]{2,1,0:T(8,128)} %get-tuple-element.7.kg_ref), custom_call_target="tpu_custom_call" | custom-call | tf_op jit(solution)/shard_map/place/pallas_call | solution.py:600

commit v4 on v3

--- a/solution.py
+++ b/solution.py
@@ -308,6 +308,26 @@
         for i, lanes in enumerate((slice(0, CH), slice(CH, TAPS)))
     ]
     stage1[0].start()
+    stage2 = []
+
+    def reduce_pair(i):
+        lanes = (slice(0, CH), slice(CH, TAPS))[i]
+        stage1[i].wait()
+        for row in range(8):
+            mine = part[row, core, :, lanes].astype(F32)
+            r1[row // 4, row % 4, :, lanes] = (mine + a1[row, :, lanes].astype(F32)).astype(BF16)
+        for o in range(1, 4):
+            copy = remote(
+                r1.at[:, (z + o) % 4, :, lanes],
+                a2.at[o - 1, :, :, lanes],
+                s2_send.at[i, o - 1],
+                s2_recv.at[i, o - 1],
+                z_peers[o - 1],
+            )
+            copy.start()
+            stage2.append(copy)
+
+    reduce_pair(0)
 
     @pl.when(t > 0)
     def _():
@@ -408,30 +428,13 @@
                     enc_copy(g, o).start()
 
     project(hid_late, 2, 0)
-    for copy in stage1:
-        copy.wait()
-    for i in range(8):
-        r1[i // 4, i % 4] = (part[i, core].astype(F32) + a1[i].astype(F32)).astype(BF16)
-    stage2 = [
-        remote(
-            r1.at[:, (z + o) % 4], a2.at[o - 1], s2_send.at[o - 1], s2_recv.at[o - 1], z_peers[o - 1]
-        )
-        for o in range(1, 4)
-    ]
-    for copy in stage2:
-        copy.start()
+    reduce_pair(1)
 
     project(hid_early, 0, 0)
     attend(0, 0)
     send_encoded(0, 0)
     attend(0, 1)
     send_encoded(0, 1)
-    project(hid_late, 2, 1)
-    project(hid_early, 0, 1)
-    attend(1, 0)
-    send_encoded(1, 0)
-    attend(1, 1)
-    send_encoded(1, 1)
     for copy in stage2:
         copy.wait()
     for i in range(2):
@@ -443,6 +446,12 @@
         ).astype(BF16)
     stage3 = remote(r2.at[1 - y], a3, s3_send.at[0], s3_recv.at[0], y_peer)
     stage3.start()
+    project(hid_late, 2, 1)
+    project(hid_early, 0, 1)
+    attend(1, 0)
+    send_encoded(1, 0)
+    attend(1, 1)
+    send_encoded(1, 1)
     stage3.wait()
     for k in range(3):
         for q in range(4):
@@ -576,8 +585,8 @@
             dma((2,)),
             dma((2,)),
             dma((2,)),
-            dma((3,)),
-            dma((3,)),
+            dma((2, 3)),
+            dma((2, 3)),
             dma((1,)),
             dma((1,)),
             dma((7,)),

time: 59.4 us -> 58.5 us (0.985); the launches traced: 59.3 us -> 57.7 us
  Pallas kernels: 58.6 us -> 57.1 us
    pallas_call x1, Pallas kernels: 56.6 us -> 55.1 us  [on_device(): pl.pallas_call(kernel, name='block', out_shape=(jax.ShapeDtypeStruct((4,...]
where the time goes in v4:
time: 58.5 us; the launch traced here: 57.7 us
  Pallas kernels  57.1 us (98%)
  between operations  0.64 us (1%)
    pallas_call x1, Pallas kernels, on_device(): pl.pallas_call(kernel, name='block', out_shape=(jax.ShapeDtypeStruct((4,...  55.1 us
    pallas_call x1, Pallas kernels, on_device(): pl.pallas_call(place, name='place', out_shape=(jax.ShapeDtypeStruct((fram...  2 us

profile of v4, /device:TPU:0, one launch (start us, length us, event | category | flops | bytes accessed | tf_op | source)
XLA Modules:
  0.0 57.7 jit_solution(14124661017178420703)
XLA Ops:
  0.6 55.1 %block.1 = (bf16[4,8,2,16,512]{4,3,2,1,0:T(8,128)(2,1)}, f32[3,32,64]{2,1,0:T(8,128)}) custom-call(bf16[4,256,512]{2,1,0:T(8,128)(2,1)} %bitcast.9, bf16[3,3,512,512]{3,2,1,0:T(8,128)(2,1)} %wsp_ref.1, bf16[1536,512]{1,0:T(8,128)(2,1)} %bitcast.7, f32[1,512]{1,0:T(1,128)} %bitcast.11, bf16[512,512]{1,0:T(8,128)(2,1)} %wq_ref.1, bf16[512,512]{1,0:T(8,128)(2,1)} %wk_ref.1, ...), custom_call_target="tpu_custom_call" | custom-call | tf_op jit(solution)/shard_map/block/pallas_call | solution.py:535
  55.7 2.0 %place.1 = (bf16[4,256,512]{2,1,0:T(8,128)(2,1)}, f32[3,32,64]{2,1,0:T(8,128)}) custom-call(bf16[4,256,512]{2,1,0:T(8,128)(2,1)} %bitcast.8, f32[3,32,64]{2,1,0:T(8,128)} %get-tuple-element.7.kg_ref), custom_call_target="tpu_custom_call" | custom-call | tf_op jit(solution)/shard_map/place/pallas_call | solution.py:609

commit v5 on v4

--- a/solution.py
+++ b/solution.py
@@ -451,7 +451,6 @@
     attend(1, 0)
     send_encoded(1, 0)
     attend(1, 1)
-    send_encoded(1, 1)
     stage3.wait()
     for k in range(3):
         for q in range(4):
@@ -469,6 +468,7 @@
     ]
     for copy in stage4:
         copy.start()
+    send_encoded(1, 1)
 
     for copy in stage4:
         copy.wait()

time: 58.5 us -> 59.4 us (1.015)
  the two profiles are of different devices: /device:TPU:0 before, /device:TPU:12 now
where the time goes in v5:
time: 59.4 us; the launch traced here: 59.2 us
  Pallas kernels  58.6 us (99%)
  between operations  0.64 us (1%)
    pallas_call x1, Pallas kernels, on_device(): pl.pallas_call(kernel, name='block', out_shape=(jax.ShapeDtypeStruct((4,...  56.6 us
    pallas_call x1, Pallas kernels, on_device(): pl.pallas_call(place, name='place', out_shape=(jax.ShapeDtypeStruct((fram...  2 us

profile of v5, /device:TPU:12, one launch (start us, length us, event | category | flops | bytes accessed | tf_op | source)
XLA Modules:
  0.0 59.2 jit_solution(192044545722896797)
XLA Ops:
  0.6 56.6 %block.1 = (bf16[4,8,2,16,512]{4,3,2,1,0:T(8,128)(2,1)}, f32[3,32,64]{2,1,0:T(8,128)}) custom-call(bf16[4,256,512]{2,1,0:T(8,128)(2,1)} %bitcast.9, bf16[3,3,512,512]{3,2,1,0:T(8,128)(2,1)} %wsp_ref.1, bf16[1536,512]{1,0:T(8,128)(2,1)} %bitcast.7, f32[1,512]{1,0:T(1,128)} %bitcast.11, bf16[512,512]{1,0:T(8,128)(2,1)} %wq_ref.1, bf16[512,512]{1,0:T(8,128)(2,1)} %wk_ref.1, ...), custom_call_target="tpu_custom_call" | custom-call | tf_op jit(solution)/shard_map/block/pallas_call | solution.py:535
  57.2 2.0 %place.1 = (bf16[4,256,512]{2,1,0:T(8,128)(2,1)}, f32[3,32,64]{2,1,0:T(8,128)}) custom-call(bf16[4,256,512]{2,1,0:T(8,128)(2,1)} %bitcast.8, f32[3,32,64]{2,1,0:T(8,128)} %get-tuple-element.7.kg_ref), custom_call_target="tpu_custom_call" | custom-call | tf_op jit(solution)/shard_map/place/pallas_call | solution.py:609
